TPU v7x, 32 devices: a whole 2x2x4 slice. The times are simulated.
32 devices in a mesh: dp: 4 (over x, core), cls: 8 (over z, y).
Axes of the slice: x: 2, y: 2, z: 4, core: 2. Of those that a mesh axis runs over, the one named last changes fastest.
Arguments:
- faces: bfloat16 [2, 32, 512], P(None, ('dp', 'cls')), may hold values from -2 to 2
- labels: int32 [2, 32], replicated, may hold values from 0 to 16383, as said below
- centres: bfloat16 [16384, 512], P(('dp', 'cls')), may hold values from -4 to 4
- momentum: bfloat16 [16384, 512], P(('dp', 'cls')), may hold values from -3 to 3
Outputs:
- face_grad: float32 [2, 32, 512], P(None, ('dp', 'cls'))
- new_centres: bfloat16 [16384, 512], P(('dp', 'cls'))
- new_momentum: bfloat16 [16384, 512], P(('dp', 'cls'))
Inputs may be any that keep to these rules, and one draw needn't show every extreme that they name: `labels`: some face has class 0 and some face has class 16384 - 1.
All inputs are finite; a program needn't handle non-finite values.
Results may differ from a plain program's by a relative error of at most 0.0057.
Values may be sent and summed in bfloat16 or wider, within the bound.
A program may use at most 64 MiB of HBM per device.

v0:
```python
import jax
import jax.numpy as jnp
from jax import lax
from jax.sharding import PartitionSpec as P

SCALE = 30.0
MARGIN = 0.4
POS_WEIGHT = 0.7
BIAS = 6.5
EPS = 1e-06
MOMENTUM_RATE = 0.9
LEARN_RATE = 0.1
DECAY = 0.0005


def as_sent(x):

    def short(part):
        return part.astype(jnp.bfloat16) if part.dtype == jnp.float32 else part

    return jax.tree.map(short, x)


def logit_grad(cosine, positive):
    halfway = (cosine + 1.0) * 0.5
    shaped = 2.0 * halfway * halfway * halfway - 1.0
    slopes = 3.0 * halfway * halfway
    pos_term = -POS_WEIGHT * SCALE * jax.nn.sigmoid(-(SCALE * (shaped - MARGIN) + BIAS))
    neg_term = (1.0 - POS_WEIGHT) * SCALE * jax.nn.sigmoid(SCALE * (shaped + MARGIN) + BIAS)
    return (jnp.where(positive, pos_term, neg_term) * slopes).astype(jnp.bfloat16)


def normalize(centres):
    master = centres.astype(jnp.float32)
    length = jnp.sqrt(jnp.sum(master * master, axis=1, keepdims=True) + EPS)
    return (master, length, master / length)


def update(master, length, unit_wide, grad_unit, momentum):
    radial = jnp.sum(unit_wide * grad_unit, axis=1, keepdims=True)
    grad_centre = (grad_unit - unit_wide * radial) / length
    velocity = MOMENTUM_RATE * momentum.astype(jnp.float32) + grad_centre + DECAY * master
    return ((master - LEARN_RATE * velocity).astype(jnp.bfloat16), velocity.astype(jnp.bfloat16))


def fold_faces(pieces, folder, start_carry):
    grouped = jax.tree.map(
        lambda part, own: part.astype(own.dtype),
        lax.all_gather(as_sent(pieces), "cls", axis=0, tiled=True),
        pieces,
    )
    return folder(
        start_carry,
        jax.tree.map(lambda part: lax.all_gather(part, "dp", axis=0, tiled=True), as_sent(grouped)),
        jnp.int32(0),
    )


def spread_back(term, face_rows):
    group_rows = lax.psum_scatter(
        term(jnp.int32(0), face_rows * lax.axis_size("cls") * lax.axis_size("dp")).astype(
            jnp.bfloat16
        ),
        "dp",
        scatter_dimension=0,
        tiled=True,
    ).astype(jnp.float32)
    return lax.psum_scatter(group_rows, "cls", scatter_dimension=0, tiled=True)


def local(faces, labels, centres, momentum):
    cls_rows = centres.shape[0]
    width = centres.shape[1]
    batches = faces.shape[0]
    face_rows = faces.shape[1]
    total_rows = labels.shape[1]
    master, length, unit_wide = normalize(centres)
    unit_rows = unit_wide.astype(jnp.bfloat16)
    class_ids = lax.axis_index(("dp", "cls")) * cls_rows + jnp.arange(cls_rows, dtype=jnp.int32)

    def make_fold(label_sets):

        def folder(carry, pieces, start):
            grad_unit, slope_sets = carry
            new_sets = []
            for label_set, piece, slope_set in zip(label_sets, pieces, slope_sets):
                cosine = lax.dot_general(
                    piece, unit_rows, (((1,), (1,)), ((), ())), preferred_element_type=jnp.float32
                )
                positive = label_set[:, None] == class_ids[None, :]
                dlogit = logit_grad(cosine, positive)
                grad_unit = grad_unit + lax.dot_general(
                    dlogit, piece, (((0,), (0,)), ((), ())), preferred_element_type=jnp.float32
                )
                new_sets.append(dlogit)
            return (grad_unit, tuple(new_sets))

        return folder

    empty_grad = jnp.zeros((cls_rows, width), jnp.float32)
    empty_slope = jnp.zeros((total_rows, cls_rows), jnp.bfloat16)
    face_sets = tuple((faces[batch_number] for batch_number in range(batches)))
    label_sets = tuple((labels[batch_number] for batch_number in range(batches)))
    empty_sets = tuple((empty_slope for batch_number in range(batches)))
    grad_unit, slope_sets = fold_faces(face_sets, make_fold(label_sets), (empty_grad, empty_sets))

    def term(start, count):
        return jnp.concatenate(
            [
                jnp.dot(slope_set, unit_rows, preferred_element_type=jnp.float32)
                for slope_set in slope_sets
            ],
            axis=1,
        )

    joined = spread_back(term, face_rows)
    face_grad = joined.reshape(face_rows, batches, width).transpose(1, 0, 2)
    new_centres, new_momentum = update(master, length, unit_wide, grad_unit, momentum)
    return (face_grad, new_centres, new_momentum)


def solution(mesh):
    in_specs = (P(None, ("dp", "cls"), None), P(), P(("dp", "cls"), None), P(("dp", "cls"), None))
    out_specs = (P(None, ("dp", "cls"), None), P(("dp", "cls"), None), P(("dp", "cls"), None))
    return jax.shard_map(local, mesh=mesh, in_specs=in_specs, out_specs=out_specs, check_vma=False)
```

profile of v0, /device:TPU:0, one launch (start us, length us, event | category | flops | bytes accessed | tf_op | source)
XLA Modules:
  0.0 139.6 jit_solution(18151039587848830202)
XLA Ops:
  7.2 0.7 copy-done.2
  7.9 0.7 copy-done.1
  8.6 27.9 %all-gather = bf16[8,1,512]{2,1,0:T(2,128)(2,1)S(1)} all-gather(bf16[1,1,512]{2,1,0:T(2,128)(2,1)S(1)} %get-tuple-element.14), channel_id=2, replica_groups=mesh['dp'=4,'cls'=8] {'cls'}, dimensions={0}, use_global_device_ids=true | all-gather | bytes 9216 | tf_op jit(solution)/shard_map/all_gather | solution.py:49
  36.5 26.1 %all-gather.2 = bf16[8,1,512]{2,1,0:T(2,128)(2,1)S(1)} all-gather(bf16[1,1,512]{2,1,0:T(2,128)(2,1)S(1)} %get-tuple-element.15), channel_id=4, replica_groups=mesh['dp'=4,'cls'=8] {'cls'}, dimensions={0}, use_global_device_ids=true | all-gather | bytes 9216 | tf_op jit(solution)/shard_map/all_gather | solution.py:49
  62.6 5.2 %all-gather.3 = bf16[32,1,512]{2,0,1:T(8,128)(2,1)S(1)} all-gather(bf16[8,1,512]{2,0,1:T(8,128)(2,1)S(1)} %copy.23), channel_id=5, replica_groups=mesh['dp'=4,'cls'=8] {'dp'}, dimensions={0}, use_global_device_ids=true | all-gather | bytes 40960 | tf_op jit(solution)/shard_map/all_gather | solution.py:54
  67.8 5.2 %all-gather.1 = bf16[32,1,512]{2,0,1:T(8,128)(2,1)S(1)} all-gather(bf16[8,1,512]{2,0,1:T(8,128)(2,1)S(1)} %copy.21), channel_id=3, replica_groups=mesh['dp'=4,'cls'=8] {'dp'}, dimensions={0}, use_global_device_ids=true | all-gather | bytes 40960 | tf_op jit(solution)/shard_map/all_gather | solution.py:54
  73.0 1.3 copy.19
  74.5 0.3 fusion.9
  74.8 0.2 convolution_convert_fusion
  75.0 0.3 fusion.7
  75.3 0.2 convolution_convert_fusion.1
  75.5 0.6 pad_maximum_fusion
  76.2 0.3 fusion.12
  76.6 0.7 copy-done
  77.2 0.2 copy.24
  77.5 0.4 multiply_reduce_fusion
  77.9 0.4 fusion.15
  78.5 1.0 copy.27
  79.5 1.0 copy.26
  80.5 0.7 copy-done.3
  81.1 0.6 dynamic-slice
  81.7 12.1 %reduce-scatter.2.cloned.1.call-done = bf16[8,1024]{1,0:T(8,128)(2,1)} async-done(((bf16[32,1024]{1,0:T(8,128)(2,1)}), bf16[8,1024]{1,0:T(8,128)(2,1)}) %reduce-scatter.2.cloned.1.call-update) | async-done | bytes 16400 | tf_op jit(solution)/shard_map/reduce_scatter | solution.py:60
  93.8 37.8 %all-reduce = f32[8,1024]{1,0:T(8,128)S(1)} all-reduce(bf16[8,1024]{1,0:T(8,128)(2,1)} %reduce-scatter.2.cloned.1.call-done), channel_id=7, replica_groups=mesh['dp'=4,'cls'=8] {'cls'}, use_global_device_ids=true, to_apply=%region_2.3.clone | all-reduce | flops 8192 | bytes 49152
  131.6 1.2 constant_dynamic-slice_fusion
  (15 shorter events, 0.6 us)
Async XLA Ops:
  7.2 86.6 %reduce-scatter.2.cloned.1.call-start = ((), (), s32[]{:S(2)}) async-start(), calls=%async_computation.1 | async-start | bytes 81920 | tf_op jit(solution)/shard_map/reduce_scatter | solution.py:60
  7.2 0.7 copy-start.2
  7.9 0.7 copy-start.1
  76.2 1.0 copy-start
  80.5 0.7 copy-start.3
Sparse Core Ops, SparseCore 0:
  76.3 17.4 reduce-scatter.1
where the time goes:
time: 140 us
  blocking collectives  102 us (73%)
  between operations  14.1 us (10%)
  waiting for transfers between devices  12.1 us (9%)
  local copies, waits for them, and re-layouts  7.99 us (6%)
  matrix products  1.74 us (1%)
  other arithmetic  1.51 us (1%)
    all_gather x2, blocking collectives, fold_faces(): lax.all_gather(as_sent(pieces), 'cls', axis=0, tiled=True)  54 us
    unnamed x1, blocking collectives  37.8 us
    reduce_scatter x1, waiting for transfers between devices, spread_back(): lax.psum_scatter(term(jnp.int32(0), face_rows * lax.axis_size('cls') * la...  12.1 us
    all_gather x2, blocking collectives, fold_faces(): lax.all_gather(part, 'dp', axis=0, tiled=True)  10.3 us
    unnamed x15, local copies, waits for them, and re-layouts  7.98 us
  transfers between devices with their start and end apart: 1, of which 1 were waited for; matrix products, arithmetic and copies ran while one was open for 3% of the time, Pallas kernels for 0%

commit v1 on v0

--- a/solution.py
+++ b/solution.py
@@ -11,6 +11,18 @@
 MOMENTUM_RATE = 0.9
 LEARN_RATE = 0.1
 DECAY = 0.0005
+
+
+def collect(x, axis, dim):
+    ways, here = (lax.axis_size(axis), lax.axis_index(axis))
+    grown, reach = (x, 1)
+    while reach < ways:
+        theirs = lax.ppermute(grown, axis, [(d, d ^ reach) for d in range(ways)])
+        mine_first = jnp.concatenate([grown, theirs], axis=dim)
+        theirs_first = jnp.concatenate([theirs, grown], axis=dim)
+        grown = jnp.where(here & reach == 0, mine_first, theirs_first)
+        reach = 2 * reach
+    return grown
 
 
 def as_sent(x):
@@ -51,7 +63,7 @@
     )
     return folder(
         start_carry,
-        jax.tree.map(lambda part: lax.all_gather(part, "dp", axis=0, tiled=True), as_sent(grouped)),
+        jax.tree.map(lambda part: collect(part, "dp", 0), as_sent(grouped)),
         jnp.int32(0),
     )
 

time: 140 us -> 136 us (0.971)
  blocking collectives: 102 us -> 91.8 us
  waiting for transfers between devices: 12.1 us -> 16.1 us
  starting transfers between devices: 0.04 us -> 2.2 us
    all_gather x2 -> x0, blocking collectives: 10.3 us -> none  [fold_faces(): lax.all_gather(part, 'dp', axis=0, tiled=True)]
    ppermute x0 -> x4, waiting for transfers between devices: none -> 2.71 us  [collect(): theirs = lax.ppermute(grown, axis, [(d, d ^ reach) for d in range(ways)])]
    ppermute x0 -> x4, starting transfers between devices: none -> 2.16 us  [collect(): theirs = lax.ppermute(grown, axis, [(d, d ^ reach) for d in range(ways)])]
  transfers between devices with their start and end apart: 1 -> 5, of which waited for: 1 -> 3; matrix products, arithmetic and copies ran while one was open for 3% -> 4% of each run, Pallas kernels for 0% -> 0%
where the time goes in v1:
time: 136 us
  blocking collectives  91.8 us (68%)
  waiting for transfers between devices  16.1 us (12%)
  between operations  14.2 us (10%)
  local copies, waits for them, and re-layouts  8.2 us (6%)
  starting transfers between devices  2.2 us (2%)
  matrix products  1.72 us (1%)
  other arithmetic  1.46 us (1%)
    all_gather x2, blocking collectives, fold_faces(): lax.all_gather(as_sent(pieces), 'cls', axis=0, tiled=True)  54 us
    unnamed x1, blocking collectives  37.7 us
    reduce_scatter x1, waiting for transfers between devices, spread_back(): lax.psum_scatter(term(jnp.int32(0), face_rows * lax.axis_size('cls') * la...  13.4 us
    unnamed x15, local copies, waits for them, and re-layouts  8.2 us
  transfers between devices with their start and end apart: 5, of which 3 were waited for; matrix products, arithmetic and copies ran while one was open for 4% of the time, Pallas kernels for 0%

profile of v1, /device:TPU:0, one launch (start us, length us, event | category | flops | bytes accessed | tf_op | source)
XLA Modules:
  0.0 135.6 jit_solution(6765676139747799770)
XLA Ops:
  7.2 0.8 slice_bitcast_fusion.1
  8.0 27.9 %all-gather.1 = bf16[8,1,512]{2,1,0:T(2,128)(2,1)S(1)} all-gather(bf16[1,1,512]{2,1,0:T(2,128)(2,1)S(1)} %get-tuple-element.15), channel_id=3, replica_groups=mesh['dp'=4,'cls'=8] {'cls'}, dimensions={0}, use_global_device_ids=true | all-gather | bytes 9216 | tf_op jit(solution)/shard_map/all_gather | solution.py:61
  35.9 26.1 %all-gather = bf16[8,1,512]{2,1,0:T(2,128)(2,1)S(1)} all-gather(bf16[1,1,512]{2,1,0:T(2,128)(2,1)S(1)} %get-tuple-element.14), channel_id=2, replica_groups=mesh['dp'=4,'cls'=8] {'cls'}, dimensions={0}, use_global_device_ids=true | all-gather | bytes 9216 | tf_op jit(solution)/shard_map/all_gather | solution.py:61
  62.1 0.7 copy-done.1
  62.7 1.3 copy.20
  64.3 0.9 copy-done
  65.4 0.6 copy-done.2
  66.1 0.6 dynamic-slice
  66.7 1.6 %collective-permute-start.1 = (bf16[16,512]{1,0:T(8,128)(2,1)S(1)}, bf16[16,512]{1,0:T(8,128)(2,1)S(1)}, u32[]{:S(2)}, u32[]{:S(2)}) collective-permute-start(bf16[16,512]{1,0:T(8,128)(2,1)S(1)} %maximum_select_fusion.2), channel_id=1, source_target_pairs={{0,16},{8,24},{16,0},{24,8},{1,17},{9,25},{17,1},{25,9},{2,18},{10... | collective-permute-start | bytes 49160 | tf_op jit(solution)/shard_map/ppermute | solution.py:20
  68.2 0.6 collective-permute-start.3
  68.8 1.6 %collective-permute-done.1 = bf16[16,512]{1,0:T(8,128)(2,1)S(1)} collective-permute-done((bf16[16,512]{1,0:T(8,128)(2,1)S(1)}, bf16[16,512]{1,0:T(8,128)(2,1)S(1)}, u32[]{:S(2)}, u32[]{:S(2)}) %collective-permute-start.1) | collective-permute-done | bytes 16416 | tf_op jit(solution)/shard_map/ppermute | solution.py:20
  70.5 0.2 fusion.5
  71.0 1.1 collective-permute-done.3
  72.0 0.3 fusion.7
  72.3 0.3 convolution_convert_fusion
  72.6 0.6 pad_maximum_fusion
  73.2 0.3 fusion.8
  73.6 0.4 multiply_reduce_fusion
  73.9 0.4 fusion.13
  74.5 1.0 copy.25
  75.5 1.0 copy.24
  76.5 13.4 %reduce-scatter.2.cloned.1.call-done = bf16[8,1024]{1,0:T(8,128)(2,1)} async-done(((bf16[32,1024]{1,0:T(8,128)(2,1)}), bf16[8,1024]{1,0:T(8,128)(2,1)}) %reduce-scatter.2.cloned.1.call-update) | async-done | bytes 16400 | tf_op jit(solution)/shard_map/reduce_scatter | solution.py:72
  89.9 37.7 %all-reduce = f32[8,1024]{1,0:T(8,128)S(1)} all-reduce(bf16[8,1024]{1,0:T(8,128)(2,1)} %reduce-scatter.2.cloned.1.call-done), channel_id=5, replica_groups=mesh['dp'=4,'cls'=8] {'cls'}, use_global_device_ids=true, to_apply=%region_2.3.clone | all-reduce | flops 8192 | bytes 49152
  127.6 1.2 constant_dynamic-slice_fusion
  (21 shorter events, 1.0 us)
Async XLA Ops:
  7.2 82.7 %reduce-scatter.2.cloned.1.call-start = ((), (), s32[]{:S(2)}) async-start(), calls=%async_computation.1 | async-start | bytes 81920 | tf_op jit(solution)/shard_map/reduce_scatter | solution.py:72
  35.9 32.3 %collective-permute-start.2 = (bf16[8,512]{1,0:T(8,128)(2,1)S(1)}, bf16[8,512]{1,0:T(8,128)(2,1)S(1)}, u32[]{:S(2)}, u32[]{:S(2)}) collective-permute-start(bf16[8,512]{1,0:T(8,128)(2,1)S(1)} %bitcast.24), channel_id=1, source_target_pairs={{0,8},{8,0},{16,24},{24,16},{1,9},{9,1},{17,25},{25,17},{2,10},{10... | collective-permute-start | bytes 24584 | tf_op jit(solution)/shard_map/ppermute | solution.py:20
  62.0 4.6 %collective-permute-start = (bf16[8,512]{1,0:T(8,128)(2,1)S(1)}, bf16[8,512]{1,0:T(8,128)(2,1)S(1)}, u32[]{:S(2)}, u32[]{:S(2)}) collective-permute-start(bf16[8,512]{1,0:T(8,128)(2,1)S(1)} %bitcast.26), channel_id=1, source_target_pairs={{0,8},{8,0},{16,24},{24,16},{1,9},{9,1},{17,25},{25,17},{2,10},{10... | collective-permute-start | bytes 24584 | tf_op jit(solution)/shard_map/ppermute | solution.py:20
  62.0 0.7 copy-start.1
  64.2 1.0 copy-start
  65.4 0.7 copy-start.2
  66.7 3.8 %collective-permute-start.1 = (bf16[16,512]{1,0:T(8,128)(2,1)S(1)}, bf16[16,512]{1,0:T(8,128)(2,1)S(1)}, u32[]{:S(2)}, u32[]{:S(2)}) collective-permute-start(bf16[16,512]{1,0:T(8,128)(2,1)S(1)} %maximum_select_fusion.2), channel_id=1, source_target_pairs={{0,16},{8,24},{16,0},{24,8},{1,17},{9,25},{17,1},{25,9},{2,18},{10... | collective-permute-start | bytes 49160 | tf_op jit(solution)/shard_map/ppermute | solution.py:20
  68.2 3.8 %collective-permute-start.3 = (bf16[16,512]{1,0:T(8,128)(2,1)S(1)}, bf16[16,512]{1,0:T(8,128)(2,1)S(1)}, u32[]{:S(2)}, u32[]{:S(2)}) collective-permute-start(bf16[16,512]{1,0:T(8,128)(2,1)S(1)} %maximum_select_fusion.3), channel_id=1, source_target_pairs={{0,16},{8,24},{16,0},{24,8},{1,17},{9,25},{17,1},{25,9},{2,18},{10... | collective-permute-start | bytes 49160 | tf_op jit(solution)/shard_map/ppermute | solution.py:20
Sparse Core Ops, SparseCore 0:
  73.3 16.5 reduce-scatter.1
